TPU v7x, 512 devices: a whole 4x8x8 slice. The times are simulated.
512 devices in a mesh: row: 8 (over y), col: 64 (over z, x, core).
Axes of the slice: x: 4, y: 8, z: 8, core: 2. Of those that a mesh axis runs over, the one named last changes fastest.
Arguments:
- ppmi: bfloat16 [4096, 128256], P('row', 'col'), may hold values from -12000 to 12000
- basis: bfloat16 [256, 128256], P(None, 'col'), may hold values from -10 to 10
Outputs:
- left_basis: bfloat16 [256, 4096], P(None, 'row')
- right_basis: bfloat16 [256, 128256], P(None, 'col')
All inputs are finite; a program needn't handle non-finite values.
Results may differ from a plain program's by a relative error of at most 0.0045.
Values may be sent and summed in bfloat16 or wider, within the bound.
A program may use at most 128 MiB of HBM per device.

v0:
```python
import jax
import jax.numpy as jnp
from jax import lax
from jax.sharding import Mesh
from jax.sharding import PartitionSpec as P

COL = ("col_0", "col_1", "col_2")


def in_blocks(array, dim, peers):
    before, after = (array.shape[:dim], array.shape[dim + 1 :])
    return jnp.moveaxis(array.reshape(*before, peers, -1, *after), dim, 0)


def sum_at_owner(array, axis, dim):
    peers = lax.axis_size(axis)
    pieces = lax.all_to_all(in_blocks(array, dim, peers), axis, 0, 0, tiled=True)
    return jnp.sum(pieces, axis=0)


def summed_rows(array, axes, dim):
    far, near = axes
    pieces = in_blocks(array, dim, lax.axis_size(far))
    nearer = sum_at_owner(pieces, near, dim + 1)
    arrived = lax.all_to_all(nearer, far, split_axis=0, concat_axis=0, tiled=True)
    return arrived.sum(axis=0)


def rows_for(lines, peers):
    spare = -len(lines) % peers
    return jnp.pad(lines, [(0, spare)] + [(0, 0)] * (lines.ndim - 1))


def copy_for_each(array, axis):
    peers = lax.axis_size(axis)
    return lax.all_to_all(
        jnp.broadcast_to(array[None], (peers, *array.shape)), axis, 0, 0, tiled=True
    )


def joined_along(pieces, dim):
    shape = list(pieces.shape[1:])
    shape[dim] *= pieces.shape[0]
    return jnp.moveaxis(pieces, 0, dim).reshape(shape)


def gathered_by_axis(array, axes, dim):
    far, near = axes
    pieces = copy_for_each(copy_for_each(array, far), near)
    return joined_along(pieces.swapaxes(0, 1).reshape(-1, *array.shape), dim)


def nested_sum(array, axes):
    lines = array.reshape(-1, array.shape[-1])
    own = summed_rows(rows_for(lines, lax.axis_size(axes[0]) * lax.axis_size(axes[1])), axes, 0)
    whole = gathered_by_axis(own, axes, 0)
    return whole[: len(lines)].reshape(array.shape)


def of_everyone(array, axis):
    everything = copy_for_each(array, axis)
    return jnp.sum(everything, axis=0)


def local_gram(block):
    return jnp.dot(block, block.T, precision=lax.Precision.HIGHEST)


def solve_rows(gram, block):
    lower = jnp.linalg.cholesky(gram)
    solved = lax.linalg.triangular_solve(lower, block, left_side=True, lower=True)
    return solved.astype(jnp.bfloat16)


def local(ppmi, basis):
    rows_total = ppmi.shape[0] * lax.axis_size("row")
    cols_total = ppmi.shape[1] * lax.axis_size(COL)
    basis_now = basis
    left = None
    partial_value = lax.dot_general(
        basis_now, ppmi, (((1,), (1,)), ((), ())), preferred_element_type=jnp.float32
    )
    y_total = nested_sum(partial_value, (("col_0", "col_1"), "col_2"))
    gram_left = of_everyone(local_gram(y_total), "row") / rows_total
    left = solve_rows(gram_left, y_total)
    z_part = jnp.dot(left, ppmi, preferred_element_type=jnp.float32)
    z_total = lax.psum(z_part, "row")
    gram_right = nested_sum(local_gram(z_total), (("col_0", "col_1"), "col_2")) / cols_total
    basis_now = solve_rows(gram_right, z_total)
    return (left, basis_now)


def solution(mesh):
    split = Mesh(
        mesh.devices.reshape(mesh.shape["row"], 8, 4, 2), ("row", "col_0", "col_1", "col_2")
    )
    placed = (P("row", COL), P(None, COL))
    return jax.shard_map(
        local,
        mesh=split,
        in_specs=placed,
        out_specs=(P(None, "row"), P(None, COL)),
        check_vma=False,
    )
```

profile of v0, /device:TPU:1, one launch (start us, length us, event | category | flops | bytes accessed | tf_op | source)
XLA Modules:
  0.0 395.1 jit_solution(5545338627759966449)
XLA Ops:
  7.2 1.6 copy-done
  8.7 1.9 fusion.18
  10.8 0.8 copy.40
  11.7 10.4 %all-to-all-start = ((f32[2,32,4,512]{3,2,1,0:T(4,128)}), f32[2,32,4,512]{3,2,1,0:T(4,128)S(1)}, u32[]{:S(2)}, u32[]{:S(2)}) async-start(f32[2,32,4,512]{3,2,1,0:T(4,128)} %bitcast.70), calls=%async_computation | async-start | bytes 1048576 | tf_op jit(solution)/shard_map/all_to_all | solution.py:17
  22.0 1.4 all-to-all-done
  23.6 18.9 %all_to_all.49 = f32[32,4,512]{2,1,0:T(4,128)S(1)} all-to-all(f32[32,4,512]{2,1,0:T(4,128)S(1)} %reduce_sum.45), channel_id=1, replica_groups=mesh['row'=8,'col_0'=8,'col_1'=4,'col_2'=2] {'col_0','col_1'}, dimensions={0} | all-to-all | bytes 524288 | tf_op jit(solution)/shard_map/all_to_all | solution.py:25
  42.6 15.0 %all_to_all.45 = f32[32,4,512]{2,1,0:T(4,128)S(1)} all-to-all(f32[32,4,512]{2,1,0:T(4,128)S(1)} %broadcast_in_dim.10), channel_id=1, replica_groups=mesh['row'=8,'col_0'=8,'col_1'=4,'col_2'=2] {'col_0','col_1'}, dimensions={0} | all-to-all | bytes 524288 | tf_op jit(solution)/shard_map/all_to_all | solution.py:36
  57.7 7.1 %all_to_all.46 = f32[2,32,4,512]{3,2,1,0:T(4,128)S(1)} all-to-all(f32[2,32,4,512]{3,2,1,0:T(4,128)S(1)} %broadcast_in_dim.11), channel_id=1, replica_groups=mesh['row'=8,'col_0'=8,'col_1'=4,'col_2'=2] {'col_2'}, dimensions={0} | all-to-all | bytes 1048576 | tf_op jit(solution)/shard_map/all_to_all | solution.py:36
  64.7 0.9 copy.27
  65.6 1.2 reshape_reshape.11
  66.8 0.6 fusion.19
  67.5 1.5 broadcast_in_dim.12
  68.9 6.8 %all-to-all-start.4 = ((f32[8,256,256]{2,1,0:T(8,128)}), f32[8,256,256]{2,1,0:T(8,128)}, u32[]{:S(2)}, u32[]{:S(2)}) async-start(f32[8,256,256]{2,1,0:T(8,128)} %broadcast_in_dim.12), calls=%async_computation.4 | async-start | bytes 4194304 | tf_op jit(solution)/shard_map/all_to_all | solution.py:36
  76.4 47.8 %all-to-all-done.4 = f32[8,256,256]{2,1,0:T(8,128)} async-done(((f32[8,256,256]{2,1,0:T(8,128)}), f32[8,256,256]{2,1,0:T(8,128)}, u32[]{:S(2)}, u32[]{:S(2)}) %all-to-all-start.4) | async-done | bytes 2097184 | tf_op jit(solution)/shard_map/all_to_all | solution.py:36
  124.2 1.8 reduce_sum.47
  126.3 11.7 %cholesky.130 = f32[128,128]{1,0:T(8,128)S(1)} custom-call(f32[128,128]{1,0:T(8,128)S(1)} %cholesky.194), custom_call_target="Cholesky" | custom-call | tf_op jit(solution)/shard_map/jit(cholesky)/cholesky | solution.py:70
  138.1 9.8 %custom-call.17 = f32[1,128,128]{1,2,0:T(8,128)S(1)} custom-call(f32[1,128,128]{2,1,0:T(8,128)S(1)} %get-tuple-element.48), custom_call_target="InvertDiagBlocksLowerTriangular" | custom-call | tf_op jit(solution)/shard_map/jit(cholesky)/cholesky | solution.py:70
  148.4 11.7 %cholesky.147 = f32[128,128]{1,0:T(8,128)S(1)} custom-call(f32[128,128]{1,0:T(8,128)S(1)} %convolution_subtract_fusion.3), custom_call_target="Cholesky" | custom-call | tf_op jit(solution)/shard_map/jit(cholesky)/cholesky | solution.py:70
  160.1 0.7 compare_reduce_fusion.2
  162.2 4.6 %while.2 = (s32[]{:T(128)}, f32[256,256]{1,0:T(8,128)S(1)}, s32[2,2]{1,0:T(2,128)S(1)}, f32[2,128,128]{2,1,0:T(8,128)S(1)}, s32[]{:T(128)}) while((s32[]{:T(128)}, f32[256,256]{1,0:T(8,128)S(1)}, s32[2,2]{1,0:T(2,128)S(1)}, f32[2,128,128]{2,1,0:T(8,128)S(1)}, s32[]{:T(128)}) %tuple.48), condition=%wide.while_cond, body=%wide.while_body.sunk | while | flops 2 | bytes 131189 | solution.py:71
  162.8 0.7 fusion.41
  163.5 1.3 bitcast_dynamic-update-slice_fusion.4
  164.8 0.7 fusion.41
  165.5 1.3 bitcast_dynamic-update-slice_fusion.4
  166.8 19.7 %custom-call.14 = f32[2,128,128]{1,2,0:T(8,128)S(1)} custom-call(f32[2,128,128]{2,1,0:T(8,128)S(1)} %get-tuple-element.10), custom_call_target="InvertDiagBlocksLowerTriangular" | custom-call | tf_op jit(solution)/shard_map/triangular_solve | solution.py:71
  187.3 0.4 convolution_convert_fusion.1
  187.8 2.0 fusion.20
  189.8 77.2 %all-reduce.3.cloned.1.call-done = f32[256,2004]{0,1:T(8,128)} async-done(((f32[256,2004]{0,1:T(8,128)}), f32[256,2004]{0,1:T(8,128)}) %all-reduce.3.cloned.1.call-update) | async-done | bytes 2052112 | tf_op jit(solution)/shard_map/psum | solution.py:87
  267.0 5.7 %fusion.21 = f32[256,256]{1,0:T(8,128)S(1)} fusion(f32[256,2004]{0,1:T(8,128)} %all-reduce.3.cloned.1.call-done), kind=kOutput, calls=%fused_computation.63 | convolution fusion | flops 1576009728 | bytes 2314240 | tf_op jit(solution)/shard_map/dot_general | solution.py:66
  272.8 7.7 %all_to_all.47 = f32[2,32,4,256]{3,2,1,0:T(4,128)S(1)} all-to-all(f32[2,32,4,256]{3,2,1,0:T(4,128)S(1)} %bitcast.86), channel_id=1, replica_groups=mesh['row'=8,'col_0'=8,'col_1'=4,'col_2'=2] {'col_2'}, dimensions={0} | all-to-all | bytes 524288 | tf_op jit(solution)/shard_map/all_to_all | solution.py:17
  280.5 19.1 %all_to_all.50 = f32[32,4,256]{2,1,0:T(4,128)S(1)} all-to-all(f32[32,4,256]{2,1,0:T(4,128)S(1)} %reduce_sum.48), channel_id=1, replica_groups=mesh['row'=8,'col_0'=8,'col_1'=4,'col_2'=2] {'col_0','col_1'}, dimensions={0} | all-to-all | bytes 262144 | tf_op jit(solution)/shard_map/all_to_all | solution.py:25
  299.7 13.0 %all_to_all.51 = f32[32,4,256]{2,1,0:T(4,128)S(1)} all-to-all(f32[32,4,256]{2,1,0:T(4,128)S(1)} %broadcast_in_dim.14), channel_id=1, replica_groups=mesh['row'=8,'col_0'=8,'col_1'=4,'col_2'=2] {'col_0','col_1'}, dimensions={0} | all-to-all | bytes 262144 | tf_op jit(solution)/shard_map/all_to_all | solution.py:36
  312.7 6.6 %all_to_all.48 = f32[2,32,4,256]{3,2,1,0:T(4,128)S(1)} all-to-all(f32[2,32,4,256]{3,2,1,0:T(4,128)S(1)} %broadcast_in_dim.15), channel_id=1, replica_groups=mesh['row'=8,'col_0'=8,'col_1'=4,'col_2'=2] {'col_2'}, dimensions={0} | all-to-all | bytes 524288 | tf_op jit(solution)/shard_map/all_to_all | solution.py:36
  319.8 11.7 %cholesky.164 = f32[128,128]{1,0:T(8,128)S(1)} custom-call(f32[128,128]{1,0:T(8,128)S(1)} %cholesky.197), custom_call_target="Cholesky" | custom-call | tf_op jit(solution)/shard_map/jit(cholesky)/cholesky | solution.py:70
  331.5 0.7 compare_reduce_fusion.1
  332.2 9.8 %custom-call.18 = f32[1,128,128]{1,2,0:T(8,128)S(1)} custom-call(f32[1,128,128]{2,1,0:T(8,128)S(1)} %get-tuple-element.44), custom_call_target="InvertDiagBlocksLowerTriangular" | custom-call | tf_op jit(solution)/shard_map/jit(cholesky)/cholesky | solution.py:70
  342.5 11.7 %cholesky.181 = f32[128,128]{1,0:T(8,128)S(1)} custom-call(f32[128,128]{1,0:T(8,128)S(1)} %convolution_subtract_fusion.2), custom_call_target="Cholesky" | custom-call | tf_op jit(solution)/shard_map/jit(cholesky)/cholesky | solution.py:70
  354.3 0.6 compare_reduce_fusion
  356.2 4.1 %while.3 = (s32[]{:T(128)}, f32[256,256]{1,0:T(8,128)S(1)}, s32[2,2]{1,0:T(2,128)S(1)}, f32[2,128,128]{2,1,0:T(8,128)S(1)}, s32[]{:T(128)}) while((s32[]{:T(128)}, f32[256,256]{1,0:T(8,128)S(1)}, s32[2,2]{1,0:T(2,128)S(1)}, f32[2,128,128]{2,1,0:T(8,128)S(1)}, s32[]{:T(128)}) %tuple.56), condition=%wide.while_cond.1, body=%wide.while_body.1.sunk | while | flops 2 | bytes 131189 | solution.py:71
  356.3 0.7 fusion.42
  356.9 1.3 bitcast_dynamic-update-slice_fusion.5
  358.3 0.7 fusion.42
  359.0 1.3 bitcast_dynamic-update-slice_fusion.5
  360.3 19.9 %custom-call.15 = f32[2,128,128]{1,2,0:T(8,128)S(1)} custom-call(f32[2,128,128]{2,1,0:T(8,128)S(1)} %get-tuple-element.18), custom_call_target="InvertDiagBlocksLowerTriangular" | custom-call | tf_op jit(solution)/shard_map/triangular_solve | solution.py:71
  380.2 3.1 fusion.17
  383.4 1.8 convolution_subtract_fusion
  385.2 1.7 convolution_convert_fusion
  386.9 1.1 pad_maximum_fusion
  (57 shorter events, 4.2 us)
Async XLA Ops:
  7.2 1.6 copy-start
  11.7 11.7 %all-to-all-start = ((f32[2,32,4,512]{3,2,1,0:T(4,128)}), f32[2,32,4,512]{3,2,1,0:T(4,128)S(1)}, u32[]{:S(2)}, u32[]{:S(2)}) async-start(f32[2,32,4,512]{3,2,1,0:T(4,128)} %bitcast.70), calls=%async_computation | async-start | bytes 1048576 | tf_op jit(solution)/shard_map/all_to_all | solution.py:17
  68.9 55.3 %all-to-all-start.4 = ((f32[8,256,256]{2,1,0:T(8,128)}), f32[8,256,256]{2,1,0:T(8,128)}, u32[]{:S(2)}, u32[]{:S(2)}) async-start(f32[8,256,256]{2,1,0:T(8,128)} %broadcast_in_dim.12), calls=%async_computation.4 | async-start | bytes 4194304 | tf_op jit(solution)/shard_map/all_to_all | solution.py:36
  75.8 191.3 %all-reduce.3.cloned.1.call-start = ((), (), s32[]{:S(2)}) async-start(), calls=%async_computation.9 | async-start | bytes 4112384 | tf_op jit(solution)/shard_map/psum | solution.py:87
  187.8 2.0 copy-start.2
  380.2 3.1 copy-start.1
Sparse Core Ops, SparseCore 0:
  190.0 77.0 all-reduce.2
where the time goes:
time: 399 us; the launch traced here: 395 us
  waiting for transfers between devices  126 us (32%)
  other arithmetic  112 us (28%)
  blocking collectives  87.3 us (22%)
  matrix products  19.1 us (5%)
  starting transfers between devices  17.5 us (4%)
  between operations  17.2 us (4%)
  local copies, waits for them, and re-layouts  15.3 us (4%)
    psum x1, waiting for transfers between devices, local(): z_total = lax.psum(z_part, 'row')  77.2 us
    another operation x13, other arithmetic, solve_rows(): lower = jnp.linalg.cholesky(gram)  68.7 us
    all_to_all x1, waiting for transfers between devices, copy_for_each(): lax.all_to_all(jnp.broadcast_to(array[None], (peers, *array.shape)), axis...  47.8 us
    all_to_all x4, blocking collectives, copy_for_each(): lax.all_to_all(jnp.broadcast_to(array[None], (peers, *array.shape)), axis...  41.7 us
    another operation x7, other arithmetic, solve_rows(): lax.linalg.triangular_solve(lower, block, left_side=True, lower=True)  40.7 us
    all_to_all x2, blocking collectives, summed_rows(): lax.all_to_all(nearer, far, split_axis=0, concat_axis=0, tiled=True)  37.9 us
    all_to_all x1, starting transfers between devices, sum_at_owner(): lax.all_to_all(in_blocks(array, dim, peers), axis, 0, 0, tiled=True)  10.4 us
    another operation x12, local copies, waits for them, and re-layouts  8.04 us
  transfers between devices with their start and end apart: 3, of which 3 were waited for; matrix products, arithmetic and copies ran while one was open for 0% of the time, Pallas kernels for 0%

commit v1 on v0

--- a/solution.py
+++ b/solution.py
@@ -84,7 +84,11 @@
     gram_left = of_everyone(local_gram(y_total), "row") / rows_total
     left = solve_rows(gram_left, y_total)
     z_part = jnp.dot(left, ppmi, preferred_element_type=jnp.float32)
-    z_total = lax.psum(z_part, "row")
+    peers_2 = lax.axis_size("row")
+    z_total, hop = (z_part, 1)
+    while hop < peers_2:
+        z_total = z_total + lax.ppermute(z_total, "row", [(i, i ^ hop) for i in range(peers_2)])
+        hop = 2 * hop
     gram_right = nested_sum(local_gram(z_total), (("col_0", "col_1"), "col_2")) / cols_total
     basis_now = solve_rows(gram_right, z_total)
     return (left, basis_now)

time: 399 us -> 534 us (1.34)
  waiting for transfers between devices: 126 us -> 267 us
  starting transfers between devices: 17.5 us -> 33.8 us
  between operations: 17.2 us -> 3.82 us
  blocking collectives: 87.3 us -> 79.8 us
    ppermute x0 -> x3, waiting for transfers between devices: none -> 217 us  [local(): lax.ppermute(z_total, 'row', [(i, i ^ hop) for i in range(peers_2)])]
    psum x1 -> x0, waiting for transfers between devices: 77.2 us -> none  [local(): z_total = lax.psum(z_part, 'row')]
    ppermute x0 -> x3, starting transfers between devices: none -> 16.3 us  [local(): lax.ppermute(z_total, 'row', [(i, i ^ hop) for i in range(peers_2)])]
    all_to_all x2, blocking collectives: 37.9 us -> 31.6 us  [summed_rows(): lax.all_to_all(nearer, far, split_axis=0, concat_axis=0, tiled=True)]
  transfers between devices with their start and end apart: 3 -> 5, of which waited for: 3 -> 5; matrix products, arithmetic and copies ran while one was open for 0% -> 0% of each run, Pallas kernels for 0% -> 0%
where the time goes in v1:
time: 534 us; the launch traced here: 530 us
  waiting for transfers between devices  267 us (50%)
  other arithmetic  113 us (21%)
  blocking collectives  79.8 us (15%)
  starting transfers between devices  33.8 us (6%)
  local copies, waits for them, and re-layouts  16.6 us (3%)
  matrix products  15.6 us (3%)
    ppermute x3, waiting for transfers between devices, local(): lax.ppermute(z_total, 'row', [(i, i ^ hop) for i in range(peers_2)])  217 us
    another operation x13, other arithmetic, solve_rows(): lower = jnp.linalg.cholesky(gram)  68.7 us
    all_to_all x1, waiting for transfers between devices, copy_for_each(): lax.all_to_all(jnp.broadcast_to(array[None], (peers, *array.shape)), axis...  48.1 us
    all_to_all x4, blocking collectives, copy_for_each(): lax.all_to_all(jnp.broadcast_to(array[None], (peers, *array.shape)), axis...  41.7 us
    another operation x7, other arithmetic, solve_rows(): lax.linalg.triangular_solve(lower, block, left_side=True, lower=True)  41.2 us
    all_to_all x2, blocking collectives, summed_rows(): lax.all_to_all(nearer, far, split_axis=0, concat_axis=0, tiled=True)  31.6 us
    ppermute x3, starting transfers between devices, local(): lax.ppermute(z_total, 'row', [(i, i ^ hop) for i in range(peers_2)])  16.3 us
  transfers between devices with their start and end apart: 5, of which 5 were waited for; matrix products, arithmetic and copies ran while one was open for 0% of the time, Pallas kernels for 0%

profile of v1, /device:TPU:1, one launch (start us, length us, event | category | flops | bytes accessed | tf_op | source)
XLA Modules:
  0.0 529.7 jit_solution(13747374498108699659)
XLA Ops:
  0.6 1.6 copy-done
  2.2 1.9 fusion.19
  4.3 0.8 copy.40
  5.1 10.4 %all-to-all-start = ((f32[2,32,4,512]{3,2,1,0:T(4,128)}), f32[2,32,4,512]{3,2,1,0:T(4,128)S(1)}, u32[]{:S(2)}, u32[]{:S(2)}) async-start(f32[2,32,4,512]{3,2,1,0:T(4,128)} %bitcast.69), calls=%async_computation | async-start | bytes 1048576 | tf_op jit(solution)/shard_map/all_to_all | solution.py:17
  15.5 1.4 all-to-all-done
  17.1 18.9 %all_to_all.49 = f32[32,4,512]{2,1,0:T(4,128)S(1)} all-to-all(f32[32,4,512]{2,1,0:T(4,128)S(1)} %reduce_sum.45), channel_id=1, replica_groups=mesh['row'=8,'col_0'=8,'col_1'=4,'col_2'=2] {'col_0','col_1'}, dimensions={0} | all-to-all | bytes 524288 | tf_op jit(solution)/shard_map/all_to_all | solution.py:25
  36.1 15.0 %all_to_all.45 = f32[32,4,512]{2,1,0:T(4,128)S(1)} all-to-all(f32[32,4,512]{2,1,0:T(4,128)S(1)} %broadcast_in_dim.10), channel_id=1, replica_groups=mesh['row'=8,'col_0'=8,'col_1'=4,'col_2'=2] {'col_0','col_1'}, dimensions={0} | all-to-all | bytes 524288 | tf_op jit(solution)/shard_map/all_to_all | solution.py:36
  51.1 7.1 %all_to_all.46 = f32[2,32,4,512]{3,2,1,0:T(4,128)S(1)} all-to-all(f32[2,32,4,512]{3,2,1,0:T(4,128)S(1)} %broadcast_in_dim.11), channel_id=1, replica_groups=mesh['row'=8,'col_0'=8,'col_1'=4,'col_2'=2] {'col_2'}, dimensions={0} | all-to-all | bytes 1048576 | tf_op jit(solution)/shard_map/all_to_all | solution.py:36
  58.2 0.9 copy.27
  59.1 1.2 reshape_reshape.11
  60.9 1.5 broadcast_in_dim.12
  62.4 7.2 %all-to-all-start.4 = ((f32[8,256,256]{2,1,0:T(8,128)}), f32[8,256,256]{2,1,0:T(8,128)}, u32[]{:S(2)}, u32[]{:S(2)}) async-start(f32[8,256,256]{2,1,0:T(8,128)} %broadcast_in_dim.12), calls=%async_computation.4 | async-start | bytes 4194304 | tf_op jit(solution)/shard_map/all_to_all | solution.py:36
  69.9 48.1 %all-to-all-done.4 = f32[8,256,256]{2,1,0:T(8,128)} async-done(((f32[8,256,256]{2,1,0:T(8,128)}), f32[8,256,256]{2,1,0:T(8,128)}, u32[]{:S(2)}, u32[]{:S(2)}) %all-to-all-start.4) | async-done | bytes 2097184 | tf_op jit(solution)/shard_map/all_to_all | solution.py:36
  117.9 1.8 reduce_sum.47
  120.1 11.7 %cholesky.130 = f32[128,128]{1,0:T(8,128)S(1)} custom-call(f32[128,128]{1,0:T(8,128)S(1)} %cholesky.194), custom_call_target="Cholesky" | custom-call | tf_op jit(solution)/shard_map/jit(cholesky)/cholesky | solution.py:70
  131.8 9.8 %custom-call.17 = f32[1,128,128]{1,2,0:T(8,128)S(1)} custom-call(f32[1,128,128]{2,1,0:T(8,128)S(1)} %get-tuple-element.48), custom_call_target="InvertDiagBlocksLowerTriangular" | custom-call | tf_op jit(solution)/shard_map/jit(cholesky)/cholesky | solution.py:70
  142.1 11.7 %cholesky.147 = f32[128,128]{1,0:T(8,128)S(1)} custom-call(f32[128,128]{1,0:T(8,128)S(1)} %convolution_subtract_fusion.2), custom_call_target="Cholesky" | custom-call | tf_op jit(solution)/shard_map/jit(cholesky)/cholesky | solution.py:70
  153.9 0.7 compare_reduce_fusion.2
  156.0 4.1 while.2
  156.0 0.7 fusion.41
  156.7 1.3 bitcast_dynamic-update-slice_fusion.4
  158.7 1.3 bitcast_dynamic-update-slice_fusion.4
  160.1 20.2 %custom-call.14 = f32[2,128,128]{1,2,0:T(8,128)S(1)} custom-call(f32[2,128,128]{2,1,0:T(8,128)S(1)} %get-tuple-element.10), custom_call_target="InvertDiagBlocksLowerTriangular" | custom-call | tf_op jit(solution)/shard_map/triangular_solve | solution.py:71
  181.5 0.7 fusion.21
  182.3 4.5 collective-permute-start
  186.8 42.5 %collective-permute-done = f32[256,2004]{0,1:T(8,128)S(1)} collective-permute-done((f32[256,2004]{0,1:T(8,128)S(1)}, f32[256,2004]{0,1:T(8,128)S(1)}, u32[]{:S(2)}, u32[]{:S(2)}) %collective-permute-start) | collective-permute-done | bytes 2052128 | tf_op jit(solution)/shard_map/ppermute | solution.py:90
  229.7 4.3 collective-permute-start.1
  234.0 87.4 %collective-permute-done.1 = f32[256,2004]{0,1:T(8,128)S(1)} collective-permute-done((f32[256,2004]{0,1:T(8,128)S(1)}, f32[256,2004]{0,1:T(8,128)S(1)}, u32[]{:S(2)}, u32[]{:S(2)}) %collective-permute-start.1) | collective-permute-done | bytes 2052128 | tf_op jit(solution)/shard_map/ppermute | solution.py:90
  321.7 7.4 %collective-permute-start.2 = (f32[256,2004]{0,1:T(8,128)S(1)}, f32[256,2004]{0,1:T(8,128)S(1)}, u32[]{:S(2)}, u32[]{:S(2)}) collective-permute-start(f32[256,2004]{0,1:T(8,128)S(1)} %add.30), channel_id=1, source_target_pairs={{0,256},{64,320},{128,384},{192,448},{256,0},{320,64},{384,128},{4... | collective-permute-start | bytes 6156296 | tf_op jit(solution)/shard_map/ppermute | solution.py:90
  329.1 87.5 %collective-permute-done.2 = f32[256,2004]{0,1:T(8,128)S(1)} collective-permute-done((f32[256,2004]{0,1:T(8,128)S(1)}, f32[256,2004]{0,1:T(8,128)S(1)}, u32[]{:S(2)}, u32[]{:S(2)}) %collective-permute-start.2) | collective-permute-done | bytes 2052128 | tf_op jit(solution)/shard_map/ppermute | solution.py:90
  417.0 1.3 copy-done.1
  418.3 3.5 fusion.22
  421.9 6.5 %all_to_all.47 = f32[2,32,4,256]{3,2,1,0:T(4,128)S(1)} all-to-all(f32[2,32,4,256]{3,2,1,0:T(4,128)S(1)} %bitcast.85), channel_id=1, replica_groups=mesh['row'=8,'col_0'=8,'col_1'=4,'col_2'=2] {'col_2'}, dimensions={0} | all-to-all | bytes 524288 | tf_op jit(solution)/shard_map/all_to_all | solution.py:17
  428.4 12.7 %all_to_all.50 = f32[32,4,256]{2,1,0:T(4,128)S(1)} all-to-all(f32[32,4,256]{2,1,0:T(4,128)S(1)} %reduce_sum.48), channel_id=1, replica_groups=mesh['row'=8,'col_0'=8,'col_1'=4,'col_2'=2] {'col_0','col_1'}, dimensions={0} | all-to-all | bytes 262144 | tf_op jit(solution)/shard_map/all_to_all | solution.py:25
  441.2 13.0 %all_to_all.51 = f32[32,4,256]{2,1,0:T(4,128)S(1)} all-to-all(f32[32,4,256]{2,1,0:T(4,128)S(1)} %broadcast_in_dim.14), channel_id=1, replica_groups=mesh['row'=8,'col_0'=8,'col_1'=4,'col_2'=2] {'col_0','col_1'}, dimensions={0} | all-to-all | bytes 262144 | tf_op jit(solution)/shard_map/all_to_all | solution.py:36
  454.2 6.6 %all_to_all.48 = f32[2,32,4,256]{3,2,1,0:T(4,128)S(1)} all-to-all(f32[2,32,4,256]{3,2,1,0:T(4,128)S(1)} %broadcast_in_dim.15), channel_id=1, replica_groups=mesh['row'=8,'col_0'=8,'col_1'=4,'col_2'=2] {'col_2'}, dimensions={0} | all-to-all | bytes 524288 | tf_op jit(solution)/shard_map/all_to_all | solution.py:36
  461.3 11.7 %cholesky.164 = f32[128,128]{1,0:T(8,128)S(1)} custom-call(f32[128,128]{1,0:T(8,128)S(1)} %cholesky.197), custom_call_target="Cholesky" | custom-call | tf_op jit(solution)/shard_map/jit(cholesky)/cholesky | solution.py:70
  473.0 0.7 compare_reduce_fusion.1
  473.7 9.8 %custom-call.18 = f32[1,128,128]{1,2,0:T(8,128)S(1)} custom-call(f32[1,128,128]{2,1,0:T(8,128)S(1)} %get-tuple-element.44), custom_call_target="InvertDiagBlocksLowerTriangular" | custom-call | tf_op jit(solution)/shard_map/jit(cholesky)/cholesky | solution.py:70
  484.0 11.7 %cholesky.181 = f32[128,128]{1,0:T(8,128)S(1)} custom-call(f32[128,128]{1,0:T(8,128)S(1)} %convolution_subtract_fusion.1), custom_call_target="Cholesky" | custom-call | tf_op jit(solution)/shard_map/jit(cholesky)/cholesky | solution.py:70
  497.7 4.1 while.3
  498.4 1.3 bitcast_dynamic-update-slice_fusion.5
  500.5 1.3 bitcast_dynamic-update-slice_fusion.5
  501.8 19.9 %custom-call.15 = f32[2,128,128]{1,2,0:T(8,128)S(1)} custom-call(f32[2,128,128]{2,1,0:T(8,128)S(1)} %get-tuple-element.18), custom_call_target="InvertDiagBlocksLowerTriangular" | custom-call | tf_op jit(solution)/shard_map/triangular_solve | solution.py:71
  521.7 3.1 fusion.18
  524.9 1.8 fusion.4
  526.6 1.8 convolution_convert_fusion
  528.4 1.1 pad_maximum_fusion
  (65 shorter events, 8.5 us)
Async XLA Ops:
  0.6 1.6 copy-start
  5.1 11.7 %all-to-all-start = ((f32[2,32,4,512]{3,2,1,0:T(4,128)}), f32[2,32,4,512]{3,2,1,0:T(4,128)S(1)}, u32[]{:S(2)}, u32[]{:S(2)}) async-start(f32[2,32,4,512]{3,2,1,0:T(4,128)} %bitcast.69), calls=%async_computation | async-start | bytes 1048576 | tf_op jit(solution)/shard_map/all_to_all | solution.py:17
  62.4 55.6 %all-to-all-start.4 = ((f32[8,256,256]{2,1,0:T(8,128)}), f32[8,256,256]{2,1,0:T(8,128)}, u32[]{:S(2)}, u32[]{:S(2)}) async-start(f32[8,256,256]{2,1,0:T(8,128)} %broadcast_in_dim.12), calls=%async_computation.4 | async-start | bytes 4194304 | tf_op jit(solution)/shard_map/all_to_all | solution.py:36
  181.5 0.7 copy-start.3
  182.3 47.0 %collective-permute-start = (f32[256,2004]{0,1:T(8,128)S(1)}, f32[256,2004]{0,1:T(8,128)S(1)}, u32[]{:S(2)}, u32[]{:S(2)}) collective-permute-start(f32[256,2004]{0,1:T(8,128)S(1)} %fusion.21), channel_id=1, source_target_pairs={{0,64},{64,0},{128,192},{192,128},{256,320},{320,256},{384,448},{4... | collective-permute-start | bytes 6156296 | tf_op jit(solution)/shard_map/ppermute | solution.py:90
  229.7 91.7 %collective-permute-start.1 = (f32[256,2004]{0,1:T(8,128)S(1)}, f32[256,2004]{0,1:T(8,128)S(1)}, u32[]{:S(2)}, u32[]{:S(2)}) collective-permute-start(f32[256,2004]{0,1:T(8,128)S(1)} %add.29), channel_id=1, source_target_pairs={{0,128},{64,192},{128,0},{192,64},{256,384},{320,448},{384,256},{4... | collective-permute-start | bytes 6156296 | tf_op jit(solution)/shard_map/ppermute | solution.py:90
  321.7 94.9 %collective-permute-start.2 = (f32[256,2004]{0,1:T(8,128)S(1)}, f32[256,2004]{0,1:T(8,128)S(1)}, u32[]{:S(2)}, u32[]{:S(2)}) collective-permute-start(f32[256,2004]{0,1:T(8,128)S(1)} %add.30), channel_id=1, source_target_pairs={{0,256},{64,320},{128,384},{192,448},{256,0},{320,64},{384,128},{4... | collective-permute-start | bytes 6156296 | tf_op jit(solution)/shard_map/ppermute | solution.py:90
  417.0 1.3 copy-start.1
  521.7 4.9 copy-start.2
